TPU v7x, 256 devices: a whole 4x4x8 slice. The times are simulated.
256 devices in a mesh: seq: 32 (over x, z), head: 8 (over y, core).
Axes of the slice: x: 4, y: 4, z: 8, core: 2. Of those that a mesh axis runs over, the one named last changes fastest.
Arguments:
- tokens: bfloat16 [24576, 4096], P('seq'), may hold values from -6 to 6
- qkv_weight: bfloat16 [3, 4096, 4096], P(None, 'seq', 'head'), may hold values from -0.09375 to 0.09375
- out_weight: bfloat16 [4096, 4096], P('head', 'seq'), may hold values from -0.09375 to 0.09375
- out_gain: float32 [4096], P('head'), may hold values from 0.25 to 1.75
Outputs:
- mixed: bfloat16 [24576, 4096], P('seq', 'head')
All inputs are finite; a program needn't handle non-finite values.
Results may differ from a plain program's by a relative error of at most 0.019.
Values may be sent and summed in bfloat16 or wider, within the bound.
No kernel may reach another device: no remote copies, remote signals or barrier semaphores. Data moves between devices by JAX's collectives and lax.ppermute only.
A program may use at most 64 MiB of HBM per device.

v0:
```python
import jax
import jax.numpy as jnp
from jax import lax
from jax.sharding import PartitionSpec as P

HEAD_DIM = 128


def carried_in(array, axis, join, neutral):
    place = lax.axis_index(axis)
    gathered = lax.all_gather(array.astype(jnp.bfloat16), axis)
    state = jnp.zeros_like(array) + jnp.asarray(neutral, array.dtype)

    def one(step, state):
        return join(state, lax.dynamic_index_in_dim(gathered, step, 0, False).astype(array.dtype))

    return lax.fori_loop(0, place, one, state)


def per_device(tokens, qkv_weight, out_weight, out_gain):
    tok_rows = tokens.shape[0]
    width_dev = qkv_weight.shape[2]
    heads_dev = width_dev // HEAD_DIM

    def add_single(shard_piece):
        return jnp.dot(tokens, shard_piece, preferred_element_type=jnp.float32)

    query_part = add_single(lax.all_gather(qkv_weight[0], "seq", axis=0, tiled=True))
    key_part = add_single(lax.all_gather(qkv_weight[1], "seq", axis=0, tiled=True))
    value_part = add_single(lax.all_gather(qkv_weight[2], "seq", axis=0, tiled=True))
    projected = jnp.stack([query_part, key_part, value_part])
    projected = projected.astype(jnp.bfloat16).reshape(3, tok_rows, heads_dev, HEAD_DIM)
    query_matrix, local_key_rows, local_value_rows = (projected[0], projected[1], projected[2])
    local_state = jnp.einsum(
        "sbq,sbn->bqn", local_key_rows, local_value_rows, preferred_element_type=jnp.float32
    )
    zero_state = jnp.zeros_like(local_state)
    prefix_state_sum = carried_in(
        local_state, "seq", lambda earlier, later: earlier + later, zero_state
    )
    causal = jnp.tril(jnp.ones((tok_rows, tok_rows), dtype=bool))
    scores = jnp.einsum(
        "thk,shk->hts", query_matrix, local_key_rows, preferred_element_type=jnp.float32
    )
    scores = jnp.where(causal[None], scores, 0.0).astype(jnp.bfloat16)
    local_term = jnp.einsum(
        "hts,shv->thv", scores, local_value_rows, preferred_element_type=jnp.float32
    )
    carried_state = jnp.einsum(
        "mal,alr->mar",
        query_matrix,
        prefix_state_sum.astype(jnp.bfloat16),
        preferred_element_type=jnp.float32,
    )
    attended = local_term + carried_state
    inv_scale = lax.rsqrt(jnp.mean(attended * attended, axis=-1, keepdims=True) + 1e-06)
    normed = ((attended * inv_scale).reshape(tok_rows, width_dev) * out_gain).astype(jnp.bfloat16)
    partial_out = jnp.dot(
        normed,
        lax.all_gather(out_weight, "seq", axis=1, tiled=True),
        preferred_element_type=jnp.float32,
    )
    return lax.psum_scatter(
        partial_out.astype(jnp.bfloat16), "head", scatter_dimension=1, tiled=True
    )


def solution(mesh):
    return jax.shard_map(
        per_device,
        mesh=mesh,
        in_specs=(P("seq", None), P(None, "seq", "head"), P("head", "seq"), P("head")),
        out_specs=P("seq", "head"),
        check_vma=False,
    )
```

profile of v0, /device:TPU:1, one launch (start us, length us, event | category | flops | bytes accessed | tf_op | source)
XLA Modules:
  0.0 480.2 jit_solution(4706658048716186455)
XLA Ops:
  6.5 0.0 all-gather.12.cloned.1.call-start
  6.5 1.8 fusion.24
  8.3 0.0 all-gather.12.cloned.1.call-update
  8.3 0.0 all-gather.16.cloned.1.call-start
  8.4 0.7 all-gather.16.cloned.1.call-update
  9.1 0.0 all-gather.14.cloned.1.call-start
  9.1 0.7 all-gather.14.cloned.1.call-update
  9.8 0.0 all-gather.18.cloned.1.call-start
  9.9 82.1 %all-gather.12.cloned.1.call-done = bf16[1,4096,512]{2,1,0:T(8,128)(2,1)} async-done(((bf16[1,128,512]{2,1,0:T(8,128)(2,1)}), bf16[1,4096,512]{2,1,0:T(8,128)(2,1)}) %all-gather.12.cloned.1.call-update) | async-done | bytes 4194320 | tf_op jit(solution)/shard_map/all_gather | solution.py:30
  91.9 7.5 %fusion.13 = bf16[768,512]{0,1:T(8,128)(2,1)S(1)} fusion(bf16[768,4096]{1,0:T(8,128)(2,1)} %param.6, bf16[1,4096,512]{2,1,0:T(8,128)(2,1)} %all-gather.12.cloned.1.call-done), kind=kOutput, calls=%fused_computation.20 | convolution fusion | flops 3221618688 | bytes 11272192 | tf_op jit(solution)/shard_map/dot_general | solution.py:26
  99.4 73.6 %all-gather.16.cloned.1.call-done = bf16[1,4096,512]{2,1,0:T(8,128)(2,1)} async-done(((bf16[1,128,512]{2,1,0:T(8,128)(2,1)}), bf16[1,4096,512]{2,1,0:T(8,128)(2,1)}) %all-gather.16.cloned.1.call-update) | async-done | bytes 4194320 | tf_op jit(solution)/shard_map/all_gather | solution.py:29
  173.0 7.5 %fusion.19 = bf16[768,512]{0,1:T(8,128)(2,1)S(1)} fusion(bf16[768,4096]{1,0:T(8,128)(2,1)} %param.6, bf16[1,4096,512]{2,1,0:T(8,128)(2,1)} %all-gather.16.cloned.1.call-done), kind=kOutput, calls=%fused_computation.22 | convolution fusion | flops 3221618688 | bytes 11272192 | tf_op jit(solution)/shard_map/dot_general | solution.py:26
  180.5 0.0 copy-start
  180.5 0.9 copy-done
  181.4 1.0 convolution_convert_fusion.1
  182.4 0.0 all-gather.18.cloned.1.call-update
  182.4 0.0 all-gather.10.cloned.1.call-start
  182.5 0.5 all-gather.10.cloned.1.call-update
  183.0 0.2 reduce-scatter.2.cloned.1.call-start
  183.3 1.0 iota_compare_fusion
  184.3 69.9 %all-gather.14.cloned.1.call-done = bf16[1,4096,512]{2,1,0:T(8,128)(2,1)} async-done(((bf16[1,128,512]{2,1,0:T(8,128)(2,1)}), bf16[1,4096,512]{2,1,0:T(8,128)(2,1)}) %all-gather.14.cloned.1.call-update) | async-done | bytes 4194320 | tf_op jit(solution)/shard_map/all_gather | solution.py:28
  254.2 7.5 %fusion.16 = bf16[768,512]{0,1:T(8,128)(2,1)S(1)} fusion(bf16[768,4096]{1,0:T(8,128)(2,1)} %param.6, bf16[1,4096,512]{2,1,0:T(8,128)(2,1)} %all-gather.14.cloned.1.call-done), kind=kOutput, calls=%fused_computation.21 | convolution fusion | flops 3221618688 | bytes 11272192 | tf_op jit(solution)/shard_map/dot_general | solution.py:26
  261.6 4.2 fusion
  265.9 69.3 %all-gather.18.cloned.1.call-done = bf16[128,128,128]{2,1,0:T(8,128)(2,1)} async-done(((bf16[4,128,128]{2,1,0:T(8,128)(2,1)}), bf16[128,128,128]{2,1,0:T(8,128)(2,1)}) %all-gather.18.cloned.1.call-update) | async-done | bytes 4194320 | tf_op jit(solution)/shard_map/all_gather | solution.py:11
  335.2 0.0 copy-start.1
  335.2 0.4 fusion.12
  335.6 0.1 bitcast_multiply_fusion.1
  335.8 0.1 copy-done.1
  335.9 0.1 fusion.11
  336.0 81.7 %all-gather.10.cloned.1.call-done = bf16[512,4096]{1,0:T(8,128)(2,1)} async-done(((bf16[512,128]{1,0:T(8,128)(2,1)}), bf16[512,4096]{1,0:T(8,128)(2,1)}) %all-gather.10.cloned.1.call-update) | async-done | bytes 4194320 | tf_op jit(solution)/shard_map/all_gather | solution.py:60
  417.7 7.6 %convolution_convert_fusion = bf16[768,4096]{1,0:T(8,128)(2,1)} fusion(bf16[768,512]{0,1:T(8,128)(2,1)S(1)} %fusion.11, bf16[512,4096]{1,0:T(8,128)(2,1)} %all-gather.10.cloned.1.call-done), kind=kOutput, calls=%fused_computation.2 | convolution fusion | flops 3224371200 | bytes 11272192 | tf_op jit(solution)/shard_map/dot_general | solution.py:58
  425.2 0.0 reduce-scatter.2.cloned.1.call-update
  425.2 48.1 %reduce-scatter.2.cloned.1.call-done = bf16[768,512]{1,0:T(8,128)(2,1)} async-done(((bf16[768,4096]{1,0:T(8,128)(2,1)}), bf16[768,512]{1,0:T(8,128)(2,1)}) %reduce-scatter.2.cloned.1.call-update) | async-done | bytes 786448 | tf_op jit(solution)/shard_map/reduce_scatter | solution.py:63
  (3 shorter events, 0.0 us)
Async XLA Ops:
  6.5 85.4 %all-gather.12.cloned.1.call-start = ((), (), s32[]{:S(2)}) async-start(), calls=%async_computation.3 | async-start | bytes 4325376 | tf_op jit(solution)/shard_map/all_gather | solution.py:30
  8.3 164.7 %all-gather.16.cloned.1.call-start = ((), (), s32[]{:S(2)}) async-start(), calls=%async_computation.5 | async-start | bytes 4325376 | tf_op jit(solution)/shard_map/all_gather | solution.py:29
  9.1 245.1 %all-gather.14.cloned.1.call-start = ((), (), s32[]{:S(2)}) async-start(), calls=%async_computation.4 | async-start | bytes 4325376 | tf_op jit(solution)/shard_map/all_gather | solution.py:28
  9.8 325.3 %all-gather.18.cloned.1.call-start = ((), (), s32[]{:S(2)}) async-start(), calls=%async_computation.6 | async-start | bytes 4325376 | tf_op jit(solution)/shard_map/all_gather | solution.py:11
  180.5 0.9 copy-start
  182.4 235.2 %all-gather.10.cloned.1.call-start = ((), (), s32[]{:S(2)}) async-start(), calls=%async_computation.1 | async-start | bytes 4325376 | tf_op jit(solution)/shard_map/all_gather | solution.py:60
  183.0 290.3 %reduce-scatter.2.cloned.1.call-start = ((), (), s32[]{:S(2)}) async-start(), calls=%async_computation.2 | async-start | bytes 7077888 | tf_op jit(solution)/shard_map/reduce_scatter | solution.py:63
  335.2 0.7 copy-start.1
Sparse Core Ops, SparseCore 0:
  9.9 81.9 all-gather.11
  94.5 78.4 all-gather.15
  175.6 78.4 all-gather.13
  256.6 78.4 all-gather.17
  337.4 80.1 all-gather.9
  425.4 47.8 reduce-scatter.1
where the time goes:
time: 481 us; the launch traced here: 480 us
  waiting for transfers between devices  427 us (89%)
  matrix products  35.6 us (7%)
  between operations  13.6 us (3%)
    all_gather x1, waiting for transfers between devices, per_device(): lax.all_gather(qkv_weight[2], 'seq', axis=0, tiled=True)  82.1 us
    all_gather x1, waiting for transfers between devices, per_device(): lax.all_gather(out_weight, 'seq', axis=1, tiled=True)  81.7 us
    all_gather x1, waiting for transfers between devices, per_device(): lax.all_gather(qkv_weight[1], 'seq', axis=0, tiled=True)  73.6 us
    all_gather x1, waiting for transfers between devices, per_device(): lax.all_gather(qkv_weight[0], 'seq', axis=0, tiled=True)  69.9 us
    all_gather x1, waiting for transfers between devices, carried_in(): gathered = lax.all_gather(array.astype(jnp.bfloat16), axis)  69.3 us
    reduce_scatter x1, waiting for transfers between devices, per_device(): lax.psum_scatter(partial_out.astype(jnp.bfloat16), 'head', scatter_dimens...  48.1 us
    dot_general x3, matrix products, add_single(): return jnp.dot(tokens, shard_piece, preferred_element_type=jnp.float32)  22.4 us
  transfers between devices with their start and end apart: 6, of which 6 were waited for; matrix products, arithmetic and copies ran while one was open for 6% of the time, Pallas kernels for 0%

commit v1 on v0

--- a/solution.py
+++ b/solution.py
@@ -27,7 +27,11 @@
 
     query_part = add_single(lax.all_gather(qkv_weight[0], "seq", axis=0, tiled=True))
     key_part = add_single(lax.all_gather(qkv_weight[1], "seq", axis=0, tiled=True))
-    value_part = add_single(lax.all_gather(qkv_weight[2], "seq", axis=0, tiled=True))
+    value_part = add_single(
+        jnp.concatenate(
+            lax.all_to_all(jnp.stack([qkv_weight[2]] * lax.axis_size("seq")), "seq", 0, 0), axis=0
+        )
+    )
     projected = jnp.stack([query_part, key_part, value_part])
     projected = projected.astype(jnp.bfloat16).reshape(3, tok_rows, heads_dev, HEAD_DIM)
     query_matrix, local_key_rows, local_value_rows = (projected[0], projected[1], projected[2])

time: 481 us -> 448 us (0.931)
  waiting for transfers between devices: 427 us -> 379 us
  starting transfers between devices: 0.38 us -> 12.3 us
    all_to_all x0 -> x1, waiting for transfers between devices: none -> 111 us  [per_device(): lax.all_to_all(jnp.stack([qkv_weight[2]] * lax.axis_size('seq')), 'seq',...]
    all_gather x1 -> x0, waiting for transfers between devices: 82.1 us -> none  [per_device(): lax.all_gather(qkv_weight[2], 'seq', axis=0, tiled=True)]
    all_gather x1, waiting for transfers between devices: 73.6 us -> 0.02 us  [per_device(): lax.all_gather(qkv_weight[1], 'seq', axis=0, tiled=True)]
    all_to_all x0 -> x1, starting transfers between devices: none -> 12 us  [per_device(): lax.all_to_all(jnp.stack([qkv_weight[2]] * lax.axis_size('seq')), 'seq',...]
  transfers between devices with their start and end apart: 6 -> 6, of which waited for: 6 -> 5; matrix products, arithmetic and copies ran while one was open for 6% -> 7% of each run, Pallas kernels for 0% -> 0%
where the time goes in v1:
time: 448 us; the launch traced here: 447 us
  waiting for transfers between devices  379 us (85%)
  matrix products  35.7 us (8%)
  between operations  13.2 us (3%)
  starting transfers between devices  12.3 us (3%)
  local copies, waits for them, and re-layouts  5.16 us (1%)
    all_to_all x1, waiting for transfers between devices, per_device(): lax.all_to_all(jnp.stack([qkv_weight[2]] * lax.axis_size('seq')), 'seq',...  111 us
    all_gather x1, waiting for transfers between devices, per_device(): lax.all_gather(out_weight, 'seq', axis=1, tiled=True)  81.7 us
    all_gather x1, waiting for transfers between devices, carried_in(): gathered = lax.all_gather(array.astype(jnp.bfloat16), axis)  69.4 us
    all_gather x1, waiting for transfers between devices, per_device(): lax.all_gather(qkv_weight[0], 'seq', axis=0, tiled=True)  67.7 us
    reduce_scatter x1, waiting for transfers between devices, per_device(): lax.psum_scatter(partial_out.astype(jnp.bfloat16), 'head', scatter_dimens...  48 us
    dot_general x3, matrix products, add_single(): return jnp.dot(tokens, shard_piece, preferred_element_type=jnp.float32)  22.4 us
    all_to_all x1, starting transfers between devices, per_device(): lax.all_to_all(jnp.stack([qkv_weight[2]] * lax.axis_size('seq')), 'seq',...  12 us
  transfers between devices with their start and end apart: 6, of which 5 were waited for; matrix products, arithmetic and copies ran while one was open for 7% of the time, Pallas kernels for 0%

profile of v1, /device:TPU:1, one launch (start us, length us, event | category | flops | bytes accessed | tf_op | source)
XLA Modules:
  0.0 447.0 jit_solution(575144732228990517)
XLA Ops:
  6.5 0.0 all-gather.12.cloned.1.call-start
  6.5 1.8 fusion.19
  8.3 0.0 all-gather.12.cloned.1.call-update
  8.3 2.4 stack.11
  10.7 12.0 %all-to-all-start = ((bf16[32,128,512]{2,1,0:T(8,128)(2,1)}), bf16[32,128,512]{2,1,0:T(8,128)(2,1)}, u32[]{:S(2)}, u32[]{:S(2)}) async-start(bf16[32,128,512]{2,1,0:T(8,128)(2,1)} %stack.11), calls=%async_computation | async-start | bytes 8388608 | tf_op jit(solution)/shard_map/all_to_all | solution.py:32
  22.7 0.0 all-gather.10.cloned.1.call-start
  22.8 0.7 all-gather.10.cloned.1.call-update
  23.5 0.0 all-gather.14.cloned.1.call-start
  23.5 111.1 %all-to-all-done = bf16[32,128,512]{2,1,0:T(8,128)(2,1)} async-done(((bf16[32,128,512]{2,1,0:T(8,128)(2,1)}), bf16[32,128,512]{2,1,0:T(8,128)(2,1)}, u32[]{:S(2)}, u32[]{:S(2)}) %all-to-all-start) | async-done | bytes 4194336 | tf_op jit(solution)/shard_map/all_to_all | solution.py:32
  134.7 7.5 %convolution_convert_fusion.1 = bf16[768,512]{0,1:T(8,128)(2,1)S(1)} fusion(bf16[768,4096]{1,0:T(8,128)(2,1)} %param.6, bf16[4096,512]{1,0:T(8,128)(2,1)} %bitcast.2), kind=kOutput, calls=%fused_computation.20 | convolution fusion | flops 3221618688 | bytes 11272192 | tf_op jit(solution)/shard_map/dot_general | solution.py:26
  142.2 0.0 all-gather.12.cloned.1.call-done
  142.2 7.5 %fusion.14 = bf16[768,512]{0,1:T(8,128)(2,1)S(1)} fusion(bf16[768,4096]{1,0:T(8,128)(2,1)} %param.6, bf16[1,4096,512]{2,1,0:T(8,128)(2,1)} %all-gather.12.cloned.1.call-done), kind=kOutput, calls=%fused_computation.19 | convolution fusion | flops 3221618688 | bytes 11272192 | tf_op jit(solution)/shard_map/dot_general | solution.py:26
  149.7 0.0 copy-start
  149.7 0.9 copy-done
  150.5 1.0 convolution_convert_fusion.2
  151.6 0.0 all-gather.14.cloned.1.call-update
  151.6 0.0 all-gather.8.cloned.1.call-start
  151.7 0.5 all-gather.8.cloned.1.call-update
  152.2 0.2 reduce-scatter.2.cloned.1.call-start
  152.4 1.0 iota_compare_fusion
  153.4 67.7 %all-gather.10.cloned.1.call-done = bf16[1,4096,512]{2,1,0:T(8,128)(2,1)} async-done(((bf16[1,128,512]{2,1,0:T(8,128)(2,1)}), bf16[1,4096,512]{2,1,0:T(8,128)(2,1)}) %all-gather.10.cloned.1.call-update) | async-done | bytes 4194320 | tf_op jit(solution)/shard_map/all_gather | solution.py:28
  221.1 7.5 %fusion.11 = bf16[768,512]{0,1:T(8,128)(2,1)S(1)} fusion(bf16[768,4096]{1,0:T(8,128)(2,1)} %param.6, bf16[1,4096,512]{2,1,0:T(8,128)(2,1)} %all-gather.10.cloned.1.call-done), kind=kOutput, calls=%fused_computation.18 | convolution fusion | flops 3221618688 | bytes 11272192 | tf_op jit(solution)/shard_map/dot_general | solution.py:26
  228.6 4.2 fusion
  232.8 69.4 %all-gather.14.cloned.1.call-done = bf16[128,128,128]{2,1,0:T(8,128)(2,1)} async-done(((bf16[4,128,128]{2,1,0:T(8,128)(2,1)}), bf16[128,128,128]{2,1,0:T(8,128)(2,1)}) %all-gather.14.cloned.1.call-update) | async-done | bytes 4194320 | tf_op jit(solution)/shard_map/all_gather | solution.py:11
  302.3 0.0 copy-start.1
  302.3 0.4 fusion.10
  302.8 0.1 bitcast_multiply_fusion.1
  302.9 0.1 copy-done.1
  303.0 0.1 fusion.9
  303.1 81.7 %all-gather.8.cloned.1.call-done = bf16[512,4096]{1,0:T(8,128)(2,1)} async-done(((bf16[512,128]{1,0:T(8,128)(2,1)}), bf16[512,4096]{1,0:T(8,128)(2,1)}) %all-gather.8.cloned.1.call-update) | async-done | bytes 4194320 | tf_op jit(solution)/shard_map/all_gather | solution.py:64
  384.8 7.6 %convolution_convert_fusion = bf16[768,4096]{1,0:T(8,128)(2,1)} fusion(bf16[768,512]{0,1:T(8,128)(2,1)S(1)} %fusion.9, bf16[512,4096]{1,0:T(8,128)(2,1)} %all-gather.8.cloned.1.call-done), kind=kOutput, calls=%fused_computation.2 | convolution fusion | flops 3224371200 | bytes 11272192 | tf_op jit(solution)/shard_map/dot_general | solution.py:62
  392.4 0.0 reduce-scatter.2.cloned.1.call-update
  392.4 48.0 %reduce-scatter.2.cloned.1.call-done = bf16[768,512]{1,0:T(8,128)(2,1)} async-done(((bf16[768,4096]{1,0:T(8,128)(2,1)}), bf16[768,512]{1,0:T(8,128)(2,1)}) %reduce-scatter.2.cloned.1.call-update) | async-done | bytes 786448 | tf_op jit(solution)/shard_map/reduce_scatter | solution.py:67
  (3 shorter events, 0.0 us)
Async XLA Ops:
  6.5 135.6 %all-gather.12.cloned.1.call-start = ((), (), s32[]{:S(2)}) async-start(), calls=%async_computation.5 | async-start | bytes 4325376 | tf_op jit(solution)/shard_map/all_gather | solution.py:29
  10.7 123.9 %all-to-all-start = ((bf16[32,128,512]{2,1,0:T(8,128)(2,1)}), bf16[32,128,512]{2,1,0:T(8,128)(2,1)}, u32[]{:S(2)}, u32[]{:S(2)}) async-start(bf16[32,128,512]{2,1,0:T(8,128)(2,1)} %stack.11), calls=%async_computation | async-start | bytes 8388608 | tf_op jit(solution)/shard_map/all_to_all | solution.py:32
  22.7 198.4 %all-gather.10.cloned.1.call-start = ((), (), s32[]{:S(2)}) async-start(), calls=%async_computation.4 | async-start | bytes 4325376 | tf_op jit(solution)/shard_map/all_gather | solution.py:28
  23.5 278.8 %all-gather.14.cloned.1.call-start = ((), (), s32[]{:S(2)}) async-start(), calls=%async_computation.6 | async-start | bytes 4325376 | tf_op jit(solution)/shard_map/all_gather | solution.py:11
  149.7 0.9 copy-start
  151.6 233.2 %all-gather.8.cloned.1.call-start = ((), (), s32[]{:S(2)}) async-start(), calls=%async_computation.2 | async-start | bytes 4325376 | tf_op jit(solution)/shard_map/all_gather | solution.py:64
  152.2 288.2 %reduce-scatter.2.cloned.1.call-start = ((), (), s32[]{:S(2)}) async-start(), calls=%async_computation.3 | async-start | bytes 7077888 | tf_op jit(solution)/shard_map/reduce_scatter | solution.py:67
  302.3 0.7 copy-start.1
Sparse Core Ops, SparseCore 0:
  9.9 131.5 all-gather.11
  144.1 76.9 all-gather.9
  223.7 78.4 all-gather.13
  304.6 80.1 all-gather.7
  392.5 47.8 reduce-scatter.1
